TPU v7x, 256 devices: a whole 4x4x8 slice. The times are simulated.
256 devices in a mesh: scen: 16 (over y, x), blk: 16 (over z, core).
Axes of the slice: x: 4, y: 4, z: 8, core: 2. Of those that a mesh axis runs over, the one named last changes fastest.
Arguments:
- link: bfloat16 [64, 256, 4096], P('scen', None, 'blk'), may hold values from -0.15625 to 0.15625
- leaf_inverse: bfloat16 [64, 256, 256], P('scen'), as said below
- leaf_rhs: float32 [64, 256], P('scen'), may hold values from -6 to 6
- node_rhs: float32 [2, 4096], P(None, 'blk'), may hold values from -6 to 6
- node_diag: float32 [2, 4096], P(None, 'blk'), may hold values from 0.5 to 4
- parent: int32 [64], P('scen'), may hold values from 0 to 1
- tile_mask: int32 [64, 16], P('scen', 'blk'), may hold values 0 or 1
Outputs:
- node_solution: float32 [2, 4096], P(None, 'blk')
- leaf_solution: float32 [64, 256], P('scen')
- schur: float32 [2, 4096, 4096], P(None, 'blk', 'scen')
Inputs may be any that keep to these rules, and one draw needn't show every extreme that they name: `leaf_inverse`: its diagonal entries lie within 1 to 2.
All inputs are finite; a program needn't handle non-finite values. No bound on the sum of `tile_mask` on one device may be relied on, other than what follows from the above.
Results may differ from a plain program's by a relative error of at most 0.0017.
Values may be sent and summed in bfloat16 or wider, within the bound.
A program may use at most 128 MiB of HBM per device.

v0:
```python
import jax
import jax.numpy as jnp
from jax import lax
from jax.sharding import PartitionSpec as P

ITERS = 4
highest = lax.Precision.HIGHEST
damping = 0.4


def body(link, leaf_inverse, leaf_rhs, node_rhs, node_diag, parent, tile_mask):
    leaf_count, width_leaf, tile_width = link.shape
    node_count = node_rhs.shape[0]
    scen_count = lax.axis_size("scen")
    blk_count = lax.axis_size("blk")
    full_width = tile_width * blk_count
    scen_index = lax.axis_index("scen")
    blk_index = lax.axis_index("blk")
    node_ids = lax.broadcasted_iota(jnp.int32, (leaf_count, node_count), 1)
    member = parent[:, None] == node_ids
    member_f = member.astype(jnp.float32)
    masked = link * tile_mask.astype(jnp.bfloat16)[:, :, None]
    solved = jnp.einsum(
        "lnm,lmc->lnc", leaf_inverse, masked, preferred_element_type=jnp.float32
    ).astype(jnp.bfloat16)
    chosen = masked[None] * member.astype(jnp.bfloat16).T[:, :, None, None]
    chosen = chosen.reshape(node_count, leaf_count * width_leaf, tile_width)
    portion = lax.all_gather(solved, "blk", axis=2, tiled=True)
    stacked = portion.reshape(leaf_count * width_leaf, portion.shape[2])
    partial_value = jnp.einsum("pkr,kc->prc", chosen, stacked, preferred_element_type=jnp.float32)
    diagonal_tile = lax.dynamic_slice_in_dim(partial_value, blk_index * tile_width, tile_width, 2)
    diag_terms = jnp.diagonal(diagonal_tile, axis1=1, axis2=2)
    inverse_f = leaf_inverse.astype(jnp.float32)
    masked_f = masked.astype(jnp.float32)
    leaf_solve = jnp.einsum("lnm,lm->ln", inverse_f, leaf_rhs, precision=highest)
    leaf_terms = jnp.einsum("lnc,ln->lc", masked_f, leaf_solve, precision=highest)
    rhs_terms = jnp.dot(member_f.T, leaf_terms, precision=highest)
    rhs_sum, diag_sum = lax.psum((rhs_terms, diag_terms), "scen")
    reduced = node_rhs - rhs_sum
    scaling = node_diag + diag_sum
    schur_rows = lax.psum_scatter(partial_value, "scen", scatter_dimension=1, tiled=True)
    schur_out = lax.all_to_all(schur_rows, "scen", split_axis=2, concat_axis=1, tiled=True)
    row_count = schur_rows.shape[1]

    def own_rows(values):
        return lax.dynamic_slice_in_dim(values, scen_index * row_count, row_count, 1)

    reduced_own = own_rows(reduced)
    scaling_own = own_rows(scaling)
    diag_own = own_rows(node_diag)

    def assemble(portion):
        gathered = lax.all_gather(portion, ("scen", "blk"), axis=1, tiled=True)
        gathered = gathered.reshape(node_count, scen_count, blk_count, row_count)
        return gathered.transpose(0, 2, 1, 3).reshape(node_count, full_width)

    portion = reduced_own / scaling_own
    for sweep in range(ITERS):
        entire = assemble(portion)
        product = diag_own * portion + jnp.einsum(
            "prc,pc->pr", schur_rows, entire, precision=highest
        )
        portion = portion + damping * (reduced_own - product) / scaling_own
    node_solution = lax.dynamic_slice_in_dim(
        assemble(portion), blk_index * tile_width, tile_width, 1
    )
    parent_values = jnp.dot(member_f, node_solution, precision=highest)
    link_term = jnp.einsum("lnc,lc->ln", masked_f, parent_values, precision=highest)
    summed = lax.psum(link_term, "blk")
    leaf_solution = jnp.einsum("lnm,lm->ln", inverse_f, leaf_rhs - summed, precision=highest)
    return (node_solution, leaf_solution, schur_out)


def solution(mesh):
    in_specs = (
        P("scen", None, "blk"),
        P("scen", None, None),
        P("scen", None),
        P(None, "blk"),
        P(None, "blk"),
        P("scen"),
        P("scen", "blk"),
    )
    out_specs = (P(None, "blk"), P("scen", None), P(None, "blk", "scen"))
    return jax.shard_map(body, mesh=mesh, in_specs=in_specs, out_specs=out_specs, check_vma=False)
```

profile of v0, /device:TPU:1, one launch (start us, length us, event | category | flops | bytes accessed | tf_op | source)
XLA Modules:
  0.0 515.3 jit_solution(16813011652913458101)
XLA Ops:
  7.2 0.0 all-gather.7.cloned.1.call-start
  7.2 0.7 convert_bitcast_fusion
  7.9 1.1 broadcast_multiply_fusion
  9.1 1.1 fusion.5
  10.3 0.0 reduce-scatter.2.cloned.1.call-start
  10.3 0.2 copy.43
  10.5 0.7 compare_convert_fusion
  11.2 59.3 %all-gather.7.cloned.1.call-done = bf16[4,256,4096]{1,2,0:T(8,128)(2,1)} async-done(((bf16[4,256,256]{1,2,0:T(8,128)(2,1)}), bf16[4,256,4096]{1,2,0:T(8,128)(2,1)}) %all-gather.7.cloned.1.call-update) | async-done | bytes 8388624 | tf_op jit(solution)/shard_map/all_gather | solution.py:28
  70.5 10.1 %fusion.2 = f32[2,256,4096]{2,1,0:T(8,128)} fusion(bf16[4,256,4096]{1,2,0:T(8,128)(2,1)} %all-gather.7.cloned.1.call-done, bf16[2,4]{1,0:T(2,128)(2,1)S(1)} %compare_convert_fusion, bf16[4,256,256]{1,2,0:T(8,128)(2,1)S(1)} %copy.43), kind=kOutput, calls=%fused_computation.3 | convolution fusion | flops 4295491584 | bytes 17301520 | tf_op jit(solution)/shard_map/pkr,kc->prc/dot_general | solution.py:30
  80.6 0.7 copy-done.2
  81.2 0.5 fusion.18
  81.8 0.3 fusion.16
  82.1 0.3 fusion.9
  82.4 1.1 constant_dynamic-slice_fusion.4
  83.5 16.4 %copy.46 = f32[2,256,256]{0,2,1:T(8,128)} copy(f32[2,256,256]{2,1,0:T(8,128)S(1)} %constant_dynamic-slice_fusion.4) | data formatting | bytes 1048576 | tf_op jit(solution)/shard_map/dynamic_slice | solution.py:31
  99.9 2.4 gather_fusion
  102.2 0.1 copy.47
  102.3 33.9 %all-reduce = (f32[2,256]{1,0:T(2,128)S(1)}, f32[2,256]{1,0:T(2,128)S(1)}) all-reduce(f32[2,256]{1,0:T(2,128)S(1)} %fusion.9, f32[2,256]{1,0:T(2,128)S(1)} %bitcast.136), channel_id=1, replica_groups=mesh['scen'=16,'blk'=16] {'scen'}, use_global_device_ids=true, to_apply=%region_0.1 | all-reduce | flops 1024 | bytes 8192 | tf_op jit(solution)/shard_map/psum | solution.py:38
  136.3 0.1 fusion.24
  136.3 65.0 %all-gather = f32[256,16,2]{1,2,0:T(2,128)S(1)} all-gather(f32[1,16,2]{1,2,0:T(2,128)S(1)} %bitcast.132), channel_id=1, replica_groups=mesh['scen'=16,'blk'=16] {'scen','blk'}, dimensions={0}, use_global_device_ids=true | all-gather | bytes 32896 | tf_op jit(solution)/shard_map/all_gather | solution.py:53
  201.4 0.2 reshape.72
  201.6 0.1 reshape.55
  201.7 0.1 copy.102
  201.8 0.1 reshape.100
  202.0 5.7 %copy.58 = f32[2,16,4096]{1,0,2:T(2,128)} copy(f32[2,16,4096]{2,1,0:T(8,128)} %reduce-scatter.2.cloned.1.call-done) | data formatting | bytes 1048576 | tf_op jit(solution)/shard_map/reduce_scatter | solution.py:41
  207.7 8.0 %reshape.107 = f32[16,1,8192]{2,1,0:T(1,128)} reshape(f32[4096,2,16]{2,1,0:T(2,128)} %bitcast.116) | data formatting | bytes 1048576
  215.6 5.3 %all-to-all-start = ((f32[16,1,8192]{2,1,0:T(1,128)}), f32[16,1,8192]{2,1,0:T(1,128)S(1)}, u32[]{:S(2)}, u32[]{:S(2)}) async-start(f32[16,1,8192]{2,1,0:T(1,128)} %reshape.107), calls=%async_computation.1 | async-start | bytes 1048576 | tf_op jit(solution)/shard_map/all_to_all | solution.py:42
  220.9 0.7 fusion.27
  221.6 0.1 divide_add_fusion.2
  221.7 62.9 %all-gather.1 = f32[256,16,2]{1,2,0:T(2,128)S(1)} all-gather(f32[1,16,2]{1,2,0:T(2,128)S(1)} %bitcast.134), channel_id=1, replica_groups=mesh['scen'=16,'blk'=16] {'scen','blk'}, dimensions={0}, use_global_device_ids=true | all-gather | bytes 32896 | tf_op jit(solution)/shard_map/all_gather | solution.py:53
  284.6 0.2 reshape.74
  284.8 0.1 reshape.57
  284.9 0.1 copy.101
  285.0 0.1 reshape.102
  285.2 0.7 fusion.28
  285.9 0.1 divide_add_fusion.1
  286.0 59.3 %all-gather.2 = f32[256,16,2]{1,2,0:T(2,128)S(1)} all-gather(f32[1,16,2]{1,2,0:T(2,128)S(1)} %bitcast.135), channel_id=1, replica_groups=mesh['scen'=16,'blk'=16] {'scen','blk'}, dimensions={0}, use_global_device_ids=true | all-gather | bytes 32896 | tf_op jit(solution)/shard_map/all_gather | solution.py:53
  345.3 0.2 reshape.76
  345.5 0.1 reshape.59
  345.6 0.1 copy.100
  345.7 0.1 reshape.104
  345.8 0.7 fusion.29
  346.5 0.1 divide_add_fusion
  346.6 59.8 %all-gather.3 = f32[256,16,2]{1,2,0:T(2,128)S(1)} all-gather(f32[1,16,2]{1,2,0:T(2,128)S(1)} %bitcast.133), channel_id=1, replica_groups=mesh['scen'=16,'blk'=16] {'scen','blk'}, dimensions={0}, use_global_device_ids=true | all-gather | bytes 32896 | tf_op jit(solution)/shard_map/all_gather | solution.py:53
  406.5 0.2 reshape.78
  406.6 0.1 reshape.61
  406.8 0.1 copy.99
  406.8 0.1 reshape.106
  407.0 0.7 fusion.30
  407.7 0.1 add_bitcast_fusion
  407.8 59.6 %all-gather.4 = f32[256,16,2]{1,2,0:T(2,128)S(1)} all-gather(f32[1,16,2]{1,2,0:T(2,128)S(1)} %add_bitcast_fusion), channel_id=1, replica_groups=mesh['scen'=16,'blk'=16] {'scen','blk'}, dimensions={0}, use_global_device_ids=true | all-gather | bytes 32896 | tf_op jit(solution)/shard_map/all_gather | solution.py:53
  467.4 0.2 reshape.80
  467.5 0.1 reshape.63
  467.7 0.1 copy.57
  467.8 0.2 reshape.64
  468.0 0.2 convolution_bitcast_fusion
  468.1 0.5 fusion.13
  468.7 23.1 %psum.23 = f32[4,256]{1,0:T(4,128)S(1)} all-reduce(f32[4,256]{1,0:T(4,128)S(1)} %bitcast.131), channel_id=1, replica_groups=mesh['scen'=16,'blk'=16] {'blk'}, use_global_device_ids=true, to_apply=%region_3.4 | all-reduce | flops 1024 | bytes 8192 | tf_op jit(solution)/shard_map/psum | solution.py:69
  491.7 0.5 fusion.11
  492.2 0.6 copy.103
  492.9 0.5 broadcast.39
  493.4 1.9 reduce
  495.3 6.9 %reshape.108 = f32[4096,2,16]{2,1,0:T(2,128)} reshape(f32[16,8192]{1,0:T(8,128)S(1)} %reduce) | data formatting | bytes 1048576
  502.2 6.3 %copy.59 = f32[2,16,16,256]{3,2,1,0:T(8,128)} copy(f32[2,16,16,256]{2,0,3,1:T(2,128)} %bitcast.115) | data formatting | bytes 1048576 | tf_op jit(solution)/shard_map/all_to_all | solution.py:42
  (27 shorter events, 0.2 us)
Async XLA Ops:
  7.2 1.9 copy-start
  7.2 63.3 %all-gather.7.cloned.1.call-start = ((), (), s32[]{:S(2)}) async-start(), calls=%async_computation.2 | async-start | bytes 8912896 | tf_op jit(solution)/shard_map/all_gather | solution.py:28
  10.3 191.7 %reduce-scatter.2.cloned.1.call-start = ((), (), s32[]{:S(2)}) async-start(), calls=%async_computation.3 | async-start | bytes 8912896 | tf_op jit(solution)/shard_map/reduce_scatter | solution.py:41
  80.6 0.7 copy-start.2
  80.6 1.5 copy-start.6
  83.4 52.8 %copy-start.3 = (f32[2,256]{1,0:T(2,128)S(1)}, f32[2,256]{1,0:T(2,128)}, u32[]{:S(2)}) copy-start(f32[2,256]{1,0:T(2,128)} %param.11) | copy-start | bytes 6148
  83.5 52.8 %copy-start.5 = (f32[2,256]{1,0:T(2,128)S(1)}, f32[2,256]{1,0:T(2,128)}, u32[]{:S(2)}) copy-start(f32[2,256]{1,0:T(2,128)} %param.10) | copy-start | bytes 6148
  202.0 19.0 %copy-start.1 = (f32[2,16,4096]{2,1,0:T(8,128)S(1)}, f32[2,16,4096]{2,1,0:T(8,128)}, u32[]{:S(2)}) copy-start(f32[2,16,4096]{2,1,0:T(8,128)} %reduce-scatter.2.cloned.1.call-done) | copy-start | bytes 1572868
  215.6 277.2 %all-to-all-start = ((f32[16,1,8192]{2,1,0:T(1,128)}), f32[16,1,8192]{2,1,0:T(1,128)S(1)}, u32[]{:S(2)}, u32[]{:S(2)}) async-start(f32[16,1,8192]{2,1,0:T(1,128)} %reshape.107), calls=%async_computation.1 | async-start | bytes 1048576 | tf_op jit(solution)/shard_map/all_to_all | solution.py:42
  468.0 40.5 %copy-start.4 = (f32[2,256]{1,0:T(2,128)}, f32[2,256]{1,0:T(2,128)S(1)}, u32[]{:S(2)}) copy-start(f32[2,256]{1,0:T(2,128)S(1)} %constant_dynamic-slice_fusion.1) | copy-start | bytes 6148
Sparse Core Ops, SparseCore 0:
  10.4 60.0 all-gather.6
  80.7 87.5 reduce-scatter.1
where the time goes:
time: 516 us; the launch traced here: 515 us
  blocking collectives  364 us (71%)
  waiting for transfers between devices  59.4 us (12%)
  local copies, waits for them, and re-layouts  51.5 us (10%)
  matrix products  16.2 us (3%)
  between operations  14.3 us (3%)
  starting transfers between devices  5.36 us (1%)
    all_gather x5, blocking collectives, assemble(): gathered = lax.all_gather(portion, ('scen', 'blk'), axis=1, tiled=True)  307 us
    all_gather x1, waiting for transfers between devices, body(): portion = lax.all_gather(solved, 'blk', axis=2, tiled=True)  59.3 us
    psum x1, blocking collectives, body(): rhs_sum, diag_sum = lax.psum((rhs_terms, diag_terms), 'scen')  33.9 us
    psum x1, blocking collectives, body(): summed = lax.psum(link_term, 'blk')  23.1 us
    dynamic_slice x2, local copies, waits for them, and re-layouts, body(): lax.dynamic_slice_in_dim(partial_value, blk_index * tile_width, tile_widt...  17.5 us
    unnamed x21, local copies, waits for them, and re-layouts  16.3 us
  transfers between devices with their start and end apart: 3, of which 1 were waited for; matrix products, arithmetic and copies ran while one was open for 6% of the time, Pallas kernels for 0%

commit v1 on v0

--- a/solution.py
+++ b/solution.py
@@ -25,7 +25,9 @@
     ).astype(jnp.bfloat16)
     chosen = masked[None] * member.astype(jnp.bfloat16).T[:, :, None, None]
     chosen = chosen.reshape(node_count, leaf_count * width_leaf, tile_width)
-    portion = lax.all_gather(solved, "blk", axis=2, tiled=True)
+    portion = jnp.concatenate(
+        lax.all_to_all(jnp.stack([solved] * lax.axis_size("blk")), "blk", 0, 0), axis=2
+    )
     stacked = portion.reshape(leaf_count * width_leaf, portion.shape[2])
     partial_value = jnp.einsum("pkr,kc->prc", chosen, stacked, preferred_element_type=jnp.float32)
     diagonal_tile = lax.dynamic_slice_in_dim(partial_value, blk_index * tile_width, tile_width, 2)

time: 516 us -> 680 us (1.32)
  waiting for transfers between devices: 59.4 us -> 183 us
  local copies, waits for them, and re-layouts: 51.5 us -> 81.4 us
  starting transfers between devices: 5.36 us -> 15.4 us
    all_to_all x0 -> x1, waiting for transfers between devices: none -> 183 us  [body(): lax.all_to_all(jnp.stack([solved] * lax.axis_size('blk')), 'blk', 0, 0)]
    all_gather x1 -> x0, waiting for transfers between devices: 59.3 us -> none  [body(): portion = lax.all_gather(solved, 'blk', axis=2, tiled=True)]
    another operation x0 -> x2, local copies, waits for them, and re-layouts: none -> 17.7 us  [the longest x1 13.5 us: body(): stacked = portion.reshape(leaf_count * width_leaf, portion.shape[2])]
    reshape x0 -> x1, local copies, waits for them, and re-layouts: none -> 11.5 us  [body(): jnp.concatenate(lax.all_to_all(jnp.stack([solved] * lax.axis_size('blk'))...]
    all_to_all x0 -> x1, starting transfers between devices: none -> 10.1 us  [body(): lax.all_to_all(jnp.stack([solved] * lax.axis_size('blk')), 'blk', 0, 0)]
    unnamed x21 -> x23, local copies, waits for them, and re-layouts: 16.3 us -> 16.4 us
  transfers between devices with their start and end apart: 3 -> 3, of which waited for: 1 -> 1; matrix products, arithmetic and copies ran while one was open for 6% -> 4% of each run, Pallas kernels for 0% -> 0%
where the time goes in v1:
time: 680 us; the launch traced here: 679 us
  blocking collectives  365 us (54%)
  waiting for transfers between devices  183 us (27%)
  local copies, waits for them, and re-layouts  81.4 us (12%)
  matrix products  15.4 us (2%)
  starting transfers between devices  15.4 us (2%)
  between operations  14.3 us (2%)
    all_gather x5, blocking collectives, assemble(): gathered = lax.all_gather(portion, ('scen', 'blk'), axis=1, tiled=True)  308 us
    all_to_all x1, waiting for transfers between devices, body(): lax.all_to_all(jnp.stack([solved] * lax.axis_size('blk')), 'blk', 0, 0)  183 us
    psum x1, blocking collectives, body(): rhs_sum, diag_sum = lax.psum((rhs_terms, diag_terms), 'scen')  34.3 us
    psum x1, blocking collectives, body(): summed = lax.psum(link_term, 'blk')  23.1 us
    dynamic_slice x2, local copies, waits for them, and re-layouts, body(): lax.dynamic_slice_in_dim(partial_value, blk_index * tile_width, tile_widt...  17.9 us
    unnamed x23, local copies, waits for them, and re-layouts  16.4 us
  transfers between devices with their start and end apart: 3, of which 1 were waited for; matrix products, arithmetic and copies ran while one was open for 4% of the time, Pallas kernels for 0%

profile of v1, /device:TPU:1, one launch (start us, length us, event | category | flops | bytes accessed | tf_op | source)
XLA Modules:
  0.0 678.8 jit_solution(16859222408671119022)
XLA Ops:
  7.2 0.7 convert_bitcast_fusion
  7.9 1.1 broadcast_multiply_fusion
  9.1 0.3 fusion
  9.4 0.2 copy.49
  9.6 4.2 stack.2
  13.8 10.1 %all-to-all-start = ((bf16[16,4,256,256]{3,2,1,0:T(8,128)(2,1)}), bf16[16,4,256,256]{3,2,1,0:T(8,128)(2,1)}, u32[]{:S(2)}, u32[]{:S(2)}) async-start(bf16[16,4,256,256]{3,2,1,0:T(8,128)(2,1)} %stack.2), calls=%async_computation | async-start | bytes 16777216 | tf_op jit(solution)/shard_map/all_to_all | solution.py:29
  24.1 0.2 copy.47
  24.3 183.0 %all-to-all-done = bf16[16,4,256,256]{3,2,1,0:T(8,128)(2,1)} async-done(((bf16[16,4,256,256]{3,2,1,0:T(8,128)(2,1)}), bf16[16,4,256,256]{3,2,1,0:T(8,128)(2,1)}, u32[]{:S(2)}, u32[]{:S(2)}) %all-to-all-start) | async-done | bytes 8388640 | tf_op jit(solution)/shard_map/all_to_all | solution.py:29
  207.3 11.5 %copy.50 = bf16[4,256,16,256]{3,2,1,0:T(8,128)(2,1)} copy(bf16[4,256,16,256]{3,1,0,2:T(8,128)(2,1)} %bitcast.7) | data formatting | bytes 16777216 | tf_op jit(solution)/shard_map/reshape | solution.py:28
  218.8 13.5 %reshape.93 = bf16[1024,4096,1]{1,0,2:T(8,128)(2,1)} reshape(bf16[4,256,16,256]{3,2,1,0:T(8,128)(2,1)} %copy.50) | data formatting | bytes 16777216 | tf_op jit(solution)/shard_map/reshape;reshape | solution.py:31
  232.3 10.0 %fusion.1 = f32[2,256,4096]{2,1,0:T(8,128)} fusion(bf16[1024,4096,1]{1,0,2:T(8,128)(2,1)} %reshape.93, bf16[2,1024]{1,0:T(2,128)(2,1)S(1)} %bitcast.143, bf16[1024,256]{0,1:T(8,128)(2,1)S(1)} %copy.47), kind=kOutput, calls=%fused_computation.4 | convolution fusion | flops 4295491584 | bytes 17305600 | tf_op jit(solution)/shard_map/pkr,kc->prc/dot_general | solution.py:32
  242.3 0.7 copy-done.2
  243.0 0.5 fusion.14
  243.5 0.3 fusion.12
  243.8 0.3 fusion.5
  244.1 1.1 constant_dynamic-slice_fusion.4
  245.2 16.8 %copy.51 = f32[2,256,256]{0,2,1:T(8,128)} copy(f32[2,256,256]{2,1,0:T(8,128)S(1)} %constant_dynamic-slice_fusion.4) | data formatting | bytes 1048576 | tf_op jit(solution)/shard_map/dynamic_slice | solution.py:33
  262.1 2.4 gather_fusion
  264.5 34.3 %all-reduce = (f32[2,256]{1,0:T(2,128)S(1)}, f32[2,256]{1,0:T(2,128)S(1)}) all-reduce(f32[2,256]{1,0:T(2,128)S(1)} %fusion.5, f32[2,256]{1,0:T(2,128)S(1)} %bitcast.137), channel_id=1, replica_groups=mesh['scen'=16,'blk'=16] {'scen'}, use_global_device_ids=true, to_apply=%region_0.1 | all-reduce | flops 1024 | bytes 8192 | tf_op jit(solution)/shard_map/psum | solution.py:40
  298.9 65.9 %all-gather = f32[256,16,2]{1,2,0:T(2,128)S(1)} all-gather(f32[1,16,2]{1,2,0:T(2,128)S(1)} %bitcast.133), channel_id=1, replica_groups=mesh['scen'=16,'blk'=16] {'scen','blk'}, dimensions={0}, use_global_device_ids=true | all-gather | bytes 32896 | tf_op jit(solution)/shard_map/all_gather | solution.py:55
  364.9 0.2 reshape.80
  365.0 0.1 reshape.63
  365.2 0.1 copy.105
  365.3 0.1 reshape.108
  365.5 5.7 copy.63
  371.2 8.0 %reshape.115 = f32[16,1,8192]{2,1,0:T(1,128)} reshape(f32[4096,2,16]{2,1,0:T(2,128)} %bitcast.116) | data formatting | bytes 1048576
  379.1 5.3 all-to-all-start.1
  384.4 0.7 fusion.23
  385.1 0.1 divide_add_fusion.2
  385.2 62.4 %all-gather.1 = f32[256,16,2]{1,2,0:T(2,128)S(1)} all-gather(f32[1,16,2]{1,2,0:T(2,128)S(1)} %bitcast.135), channel_id=1, replica_groups=mesh['scen'=16,'blk'=16] {'scen','blk'}, dimensions={0}, use_global_device_ids=true | all-gather | bytes 32896 | tf_op jit(solution)/shard_map/all_gather | solution.py:55
  447.6 0.2 reshape.82
  447.8 0.1 reshape.65
  447.9 0.1 copy.104
  448.0 0.1 reshape.110
  448.2 0.7 fusion.24
  448.9 0.1 divide_add_fusion.1
  448.9 59.8 %all-gather.2 = f32[256,16,2]{1,2,0:T(2,128)S(1)} all-gather(f32[1,16,2]{1,2,0:T(2,128)S(1)} %bitcast.136), channel_id=1, replica_groups=mesh['scen'=16,'blk'=16] {'scen','blk'}, dimensions={0}, use_global_device_ids=true | all-gather | bytes 32896 | tf_op jit(solution)/shard_map/all_gather | solution.py:55
  508.8 0.2 reshape.84
  508.9 0.1 reshape.67
  509.1 0.1 copy.103
  509.2 0.1 reshape.112
  509.3 0.7 fusion.25
  510.0 0.1 divide_add_fusion
  510.1 59.6 %all-gather.3 = f32[256,16,2]{1,2,0:T(2,128)S(1)} all-gather(f32[1,16,2]{1,2,0:T(2,128)S(1)} %bitcast.134), channel_id=1, replica_groups=mesh['scen'=16,'blk'=16] {'scen','blk'}, dimensions={0}, use_global_device_ids=true | all-gather | bytes 32896 | tf_op jit(solution)/shard_map/all_gather | solution.py:55
  569.7 0.2 reshape.86
  569.9 0.1 reshape.69
  570.0 0.1 copy.102
  570.1 0.1 reshape.114
  570.3 0.7 fusion.26
  570.9 0.1 add_bitcast_fusion
  571.0 59.8 %all-gather.4 = f32[256,16,2]{1,2,0:T(2,128)S(1)} all-gather(f32[1,16,2]{1,2,0:T(2,128)S(1)} %add_bitcast_fusion), channel_id=1, replica_groups=mesh['scen'=16,'blk'=16] {'scen','blk'}, dimensions={0}, use_global_device_ids=true | all-gather | bytes 32896 | tf_op jit(solution)/shard_map/all_gather | solution.py:55
  630.9 0.2 reshape.88
  631.0 0.1 reshape.71
  631.2 0.1 copy.62
  631.3 0.2 reshape.72
  631.4 0.2 convolution_bitcast_fusion
  631.6 0.5 fusion.9
  632.2 23.1 %psum.23 = f32[4,256]{1,0:T(4,128)S(1)} all-reduce(f32[4,256]{1,0:T(4,128)S(1)} %bitcast.132), channel_id=1, replica_groups=mesh['scen'=16,'blk'=16] {'blk'}, use_global_device_ids=true, to_apply=%region_3.4 | all-reduce | flops 1024 | bytes 8192 | tf_op jit(solution)/shard_map/psum | solution.py:71
  655.2 0.5 fusion.7
  655.7 0.6 copy.106
  656.3 0.5 broadcast.43
  656.9 1.9 reduce
  658.8 6.9 %reshape.116 = f32[4096,2,16]{2,1,0:T(2,128)} reshape(f32[16,8192]{1,0:T(8,128)S(1)} %reduce) | data formatting | bytes 1048576
  665.7 6.3 copy.64
  (32 shorter events, 0.5 us)
Async XLA Ops:
  7.2 1.9 copy-start
  13.8 10.2 %copy-start.6 = (s32[4]{0:T(128)S(1)}, s32[4]{0:T(128)}, u32[]{:S(2)}) copy-start(s32[4]{0:T(128)} %param.12) | copy-start | bytes 52
  13.8 193.5 %all-to-all-start = ((bf16[16,4,256,256]{3,2,1,0:T(8,128)(2,1)}), bf16[16,4,256,256]{3,2,1,0:T(8,128)(2,1)}, u32[]{:S(2)}, u32[]{:S(2)}) async-start(bf16[16,4,256,256]{3,2,1,0:T(8,128)(2,1)} %stack.2), calls=%async_computation | async-start | bytes 16777216 | tf_op jit(solution)/shard_map/all_to_all | solution.py:29
  24.0 341.5 %reduce-scatter.2.cloned.1.call-start = ((), (), s32[]{:S(2)}) async-start(), calls=%async_computation.3 | async-start | bytes 8912896 | tf_op jit(solution)/shard_map/reduce_scatter | solution.py:43
  242.3 0.7 copy-start.2
  245.2 53.7 %copy-start.3 = (f32[2,256]{1,0:T(2,128)S(1)}, f32[2,256]{1,0:T(2,128)}, u32[]{:S(2)}) copy-start(f32[2,256]{1,0:T(2,128)} %param.11) | copy-start | bytes 6148
  245.2 53.6 %copy-start.5 = (f32[2,256]{1,0:T(2,128)S(1)}, f32[2,256]{1,0:T(2,128)}, u32[]{:S(2)}) copy-start(f32[2,256]{1,0:T(2,128)} %param.10) | copy-start | bytes 6148
  365.4 19.0 %copy-start.1 = (f32[2,16,4096]{2,1,0:T(8,128)S(1)}, f32[2,16,4096]{2,1,0:T(8,128)}, u32[]{:S(2)}) copy-start(f32[2,16,4096]{2,1,0:T(8,128)} %reduce-scatter.2.cloned.1.call-done) | copy-start | bytes 1572868
  379.1 277.2 %all-to-all-start.1 = ((f32[16,1,8192]{2,1,0:T(1,128)}), f32[16,1,8192]{2,1,0:T(1,128)S(1)}, u32[]{:S(2)}, u32[]{:S(2)}) async-start(f32[16,1,8192]{2,1,0:T(1,128)} %reshape.115), calls=%async_computation.2 | async-start | bytes 1048576 | tf_op jit(solution)/shard_map/all_to_all | solution.py:44
  631.4 40.5 %copy-start.4 = (f32[2,256]{1,0:T(2,128)}, f32[2,256]{1,0:T(2,128)S(1)}, u32[]{:S(2)}) copy-start(f32[2,256]{1,0:T(2,128)S(1)} %constant_dynamic-slice_fusion.1) | copy-start | bytes 6148
Sparse Core Ops, SparseCore 0:
  242.5 88.8 reduce-scatter.1
